TPU v7x, 32 devices: a whole 2x2x4 slice. The times are simulated.
32 devices in a mesh: dp: 4 (over z), row: 4 (over y, x), col: 2 (over core).
Axes of the slice: x: 2, y: 2, z: 4, core: 2. Of those that a mesh axis runs over, the one named last changes fastest.
Arguments:
- tokens: bfloat16 [8, 2048, 768], P(('dp', 'col'), 'row'), may hold values from -6 to 6
- cotangent: bfloat16 [8, 2048, 768], P(('dp', 'col'), 'row'), may hold values from -6 to 6
- timesteps: int32 [8], P(('dp', 'col')), may hold values from 0 to 999
- prefix_len: int32 [8], P(('dp', 'col')), may hold values from 204 to 1024, as said below
- time_table: bfloat16 [1000, 768], P('col'), may hold values from -3 to 3
- ln1_gain: float32 [768], replicated, may hold values from 0.25 to 1.75
- ln1_bias: float32 [768], replicated, may hold values from -3 to 3
- w_qkv: bfloat16 [768, 3, 768], P('col', None, 'row'), may hold values from -0.3125 to 0.3125
- w_out: bfloat16 [768, 768], P('col', 'row'), may hold values from -1.75 to 1.75
- out_bias: float32 [768], replicated, may hold values from -3 to 3
- ln2_gain: float32 [768], replicated, may hold values from 0.25 to 1.75
- ln2_bias: float32 [768], replicated, may hold values from -3 to 3
- w_up: bfloat16 [768, 3072], P('col', 'row'), may hold values from -0.21875 to 0.21875
- up_bias: float32 [3072], P('row'), may hold values from -3 to 3
- w_down: bfloat16 [768, 3072], P('col', 'row'), may hold values from -0.109375 to 0.109375
- down_bias: float32 [768], replicated, may hold values from -4 to 4
Outputs:
- layer_out: bfloat16 [8, 2048, 768], P(('dp', 'col'), 'row')
- tokens_grad: float32 [8, 2048, 768], P(('dp', 'col'), 'row')
- table_grad: float32 [1000, 768], P('col')
- ln1_gain_grad: float32 [768], replicated
- ln1_bias_grad: float32 [768], replicated
- qkv_grad: float32 [768, 3, 768], P('col', None, 'row')
- out_grad: float32 [768, 768], P('col', 'row')
- out_bias_grad: float32 [768], replicated
- ln2_gain_grad: float32 [768], replicated
- ln2_bias_grad: float32 [768], replicated
- up_grad: float32 [768, 3072], P('col', 'row')
- up_bias_grad: float32 [3072], P('row')
- down_grad: float32 [768, 3072], P('col', 'row')
- down_bias_grad: float32 [768], replicated
Inputs may be any that keep to these rules, and one draw needn't show every extreme that they name: `prefix_len`: each sequence's prefix length lies between 204 and 1024, and some sequence takes each end.
All inputs are finite; a program needn't handle non-finite values.
Results may differ from a plain program's by a relative error of at most 0.02.
Values may be sent and summed in bfloat16 or wider, within the bound.
A program may use at most 128 MiB of HBM per device.

v0:
```python
import jax
import jax.numpy as jnp
from jax import lax
from jax.sharding import PartitionSpec as P

HD = 64
norm_eps = 1e-05
masked_score = -1e30


def gelu_exact(values):
    return jax.nn.gelu(values, approximate=False)


def gather_rows(values):
    return lax.all_gather(values, "row", axis=1, tiled=True)


def scatter_rows(values):
    return lax.psum_scatter(
        values.astype(jnp.bfloat16), "row", scatter_dimension=1, tiled=True
    ).astype(jnp.float32)


def gather_grads(values):
    return lax.all_gather(values, "row", axis=1, tiled=True)


def scatter_grads(values):
    return lax.psum_scatter(
        values.astype(jnp.bfloat16), "row", scatter_dimension=1, tiled=True
    ).astype(jnp.float32)


def norm_forward(hidden, gain_vec, bias_vec):
    width = hidden.shape[-1]
    average = jnp.sum(hidden, axis=-1, keepdims=True) / width
    variance = jnp.sum(hidden * hidden, axis=-1, keepdims=True) / width - average * average
    inverse = lax.rsqrt(variance + norm_eps)
    centred = (hidden - average) * inverse
    return (centred * gain_vec + bias_vec, centred, inverse)


def norm_backward(grad_out, centred, inverse, gain_vec):
    width = grad_out.shape[-1]
    scaled = grad_out * gain_vec
    first_mean = jnp.sum(scaled, axis=-1, keepdims=True) / width
    second_mean = jnp.sum(scaled * centred, axis=-1, keepdims=True) / width
    grad_in = inverse * (scaled - first_mean - centred * second_mean)
    return (grad_in, jnp.sum(grad_out * centred, axis=(0, 1)), jnp.sum(grad_out, axis=(0, 1)))


def attend_forward(queries, key_rows, values, prefix):
    length = queries.shape[0]
    block_rows = min(512, length)
    score_scale = queries.shape[2] ** (-0.5)
    key_pos = jnp.arange(length, dtype=jnp.int32)

    def one_block(block_index):
        row_start = block_index * block_rows
        query_blk = lax.dynamic_slice_in_dim(queries, row_start, block_rows, 0)
        scores = (
            jnp.einsum("qhd,khd->hqk", query_blk, key_rows, preferred_element_type=jnp.float32)
            * score_scale
        )
        query_pos = row_start + jnp.arange(block_rows, dtype=jnp.int32)
        allowed = (key_pos[None, :] <= query_pos[:, None]) | (key_pos[None, :] < prefix)
        scores = jnp.where(allowed[None], scores, masked_score)
        row_max = jnp.max(scores, axis=2, keepdims=True)
        exponent = jnp.exp(scores - row_max)
        row_total = jnp.sum(exponent, axis=2, keepdims=True)
        soft_low = (exponent / row_total).astype(jnp.bfloat16)
        mixed_blk = jnp.einsum("hqk,khd->qhd", soft_low, values, preferred_element_type=jnp.float32)
        return (mixed_blk, (row_max + jnp.log(row_total))[:, :, 0])

    mixed, logsums = lax.map(one_block, jnp.arange(length // block_rows, dtype=jnp.int32))
    return (mixed.reshape(queries.shape), logsums)


def attend_backward(queries, key_rows, values, mixed, logsums, grad_mixed, prefix):
    length = queries.shape[0]
    block_rows = min(512, length)
    score_scale = queries.shape[2] ** (-0.5)
    key_pos = jnp.arange(length, dtype=jnp.int32)
    delta = jnp.sum(grad_mixed.astype(jnp.float32) * mixed, axis=2)

    def one_block(grads_carry, block_index):
        grad_keys, grad_values = grads_carry
        row_start = block_index * block_rows
        query_blk = lax.dynamic_slice_in_dim(queries, row_start, block_rows, 0)
        grad_blk = lax.dynamic_slice_in_dim(grad_mixed, row_start, block_rows, 0)
        delta_blk = lax.dynamic_slice_in_dim(delta, row_start, block_rows, 0)
        scores = (
            jnp.einsum("qhd,khd->hqk", query_blk, key_rows, preferred_element_type=jnp.float32)
            * score_scale
        )
        query_pos = row_start + jnp.arange(block_rows, dtype=jnp.int32)
        allowed = (key_pos[None, :] <= query_pos[:, None]) | (key_pos[None, :] < prefix)
        scores = jnp.where(allowed[None], scores, masked_score)
        weights_soft = jnp.exp(scores - logsums[block_index][:, :, None])
        grad_soft = jnp.einsum("qhd,khd->hqk", grad_blk, values, preferred_element_type=jnp.float32)
        grad_scores = (weights_soft * (grad_soft - delta_blk.T[:, :, None])).astype(jnp.bfloat16)
        grad_query = (
            jnp.einsum("hqk,khd->qhd", grad_scores, key_rows, preferred_element_type=jnp.float32)
            * score_scale
        )
        grad_keys = (
            grad_keys
            + jnp.einsum("hqk,qhd->khd", grad_scores, query_blk, preferred_element_type=jnp.float32)
            * score_scale
        )
        grad_values = grad_values + jnp.einsum(
            "hqk,qhd->khd",
            weights_soft.astype(jnp.bfloat16),
            grad_blk,
            preferred_element_type=jnp.float32,
        )
        return ((grad_keys, grad_values), grad_query)

    zero_grads = jnp.zeros(key_rows.shape, jnp.float32)
    final_grads, grad_queries = lax.scan(
        one_block, (zero_grads, zero_grads), jnp.arange(length // block_rows, dtype=jnp.int32)
    )
    return jnp.stack([grad_queries.reshape(key_rows.shape), final_grads[0], final_grads[1]], axis=1)


def body(
    tokens,
    cotangent,
    timesteps,
    prefix_len,
    time_table,
    ln1_gain,
    ln1_bias,
    w_qkv,
    w_out,
    out_bias,
    ln2_gain,
    ln2_bias,
    w_up,
    up_bias,
    w_down,
    down_bias,
):
    highest = lax.Precision.HIGHEST
    qkv_full, out_full, up_full, down_full, table_full = (
        lax.all_gather(w_qkv, "col", axis=0, tiled=True),
        lax.all_gather(w_out, "col", axis=0, tiled=True),
        lax.all_gather(w_up, "col", axis=0, tiled=True),
        lax.all_gather(w_down, "col", axis=0, tiled=True),
        lax.all_gather(time_table, "col", axis=0, tiled=True),
    )
    seq_count = tokens.shape[0]
    width_heads = qkv_full.shape[2]
    heads_local = width_heads // HD
    picked = (
        timesteps[:, None] == jnp.arange(table_full.shape[0], dtype=jnp.int32)[None, :]
    ).astype(jnp.float32)
    embed_rows = jnp.dot(picked, table_full.astype(jnp.float32), precision=highest)

    def sequence_forward(seq_item):
        parts_seq, prefix = seq_item
        return attend_forward(parts_seq[:, 0], parts_seq[:, 1], parts_seq[:, 2], prefix)

    def forward_pass(tokens_in):
        hidden0 = tokens_in.astype(jnp.float32) + embed_rows[:, None, :]
        normed1, centred1, inverse1 = norm_forward(hidden0, ln1_gain, ln1_bias)
        full_one = gather_rows(normed1.astype(jnp.bfloat16))
        length = full_one.shape[1]
        project = jnp.einsum(
            "std,dkh->stkh", full_one, qkv_full, preferred_element_type=jnp.float32
        ).astype(jnp.bfloat16)
        parts = project.reshape(seq_count, length, 3, heads_local, HD)
        mixed, logsums = lax.map(sequence_forward, (parts, prefix_len))
        weighted = mixed.reshape(seq_count, length, width_heads).astype(jnp.bfloat16)
        branch = scatter_rows(
            jnp.einsum("sth,dh->std", weighted, out_full, preferred_element_type=jnp.float32)
        )
        hidden1 = hidden0 + (branch + out_bias)
        normed2, centred2, inverse2 = norm_forward(hidden1, ln2_gain, ln2_bias)
        full_two = gather_rows(normed2.astype(jnp.bfloat16))
        inner = (
            jnp.einsum("std,df->stf", full_two, up_full, preferred_element_type=jnp.float32)
            + up_bias
        )
        active = gelu_exact(inner).astype(jnp.bfloat16)
        result = hidden1 + (
            scatter_rows(
                jnp.einsum("stf,df->std", active, down_full, preferred_element_type=jnp.float32)
            )
            + down_bias
        )
        saved = (
            full_one,
            centred1,
            inverse1,
            parts,
            mixed,
            logsums,
            weighted,
            centred2,
            inverse2,
            full_two,
            inner,
            active,
        )
        return (result, saved)

    result, saved = forward_pass(tokens)
    (
        full_one,
        centred1,
        inverse1,
        parts,
        mixed,
        logsums,
        weighted,
        centred2,
        inverse2,
        full_two,
        inner,
        active,
    ) = saved
    length = full_one.shape[1]
    grad_full = gather_grads(cotangent)
    down_grad_full = jnp.einsum(
        "std,stf->df", grad_full, active, preferred_element_type=jnp.float32
    )
    grad_active = jnp.einsum(
        "std,df->stf", grad_full, down_full, preferred_element_type=jnp.float32
    )
    unused_out, gelu_back = jax.vjp(gelu_exact, inner)
    grad_inner = gelu_back(grad_active)[0]
    inner_low = grad_inner.astype(jnp.bfloat16)
    up_grad_full = jnp.einsum(
        "std,stf->df", full_two, inner_low, preferred_element_type=jnp.float32
    )
    grad_normed2 = scatter_grads(
        jnp.einsum("stf,df->std", inner_low, up_full, preferred_element_type=jnp.float32)
    )
    grad_norm_two, ln2_gain_part, ln2_bias_part = norm_backward(
        grad_normed2, centred2, inverse2, ln2_gain
    )
    grad_hidden1 = cotangent.astype(jnp.float32) + grad_norm_two
    grad_branch_full = gather_grads(grad_hidden1.astype(jnp.bfloat16))
    out_grad_full = jnp.einsum(
        "std,sth->dh", grad_branch_full, weighted, preferred_element_type=jnp.float32
    )
    grad_weighted = jnp.einsum(
        "std,dh->sth", grad_branch_full, out_full, preferred_element_type=jnp.float32
    ).astype(jnp.bfloat16)

    def sequence_backward(seq_item):
        parts_seq, mixed_seq, logsum_seq, grad_seq, prefix = seq_item
        return attend_backward(
            parts_seq[:, 0],
            parts_seq[:, 1],
            parts_seq[:, 2],
            mixed_seq,
            logsum_seq,
            grad_seq,
            prefix,
        )

    grad_parts = lax.map(
        sequence_backward,
        (
            parts,
            mixed,
            logsums,
            grad_weighted.reshape(seq_count, length, heads_local, HD),
            prefix_len,
        ),
    )
    grad_project = grad_parts.reshape(seq_count, length, 3, width_heads).astype(jnp.bfloat16)
    qkv_grad_full = jnp.einsum(
        "std,stkh->dkh", full_one, grad_project, preferred_element_type=jnp.float32
    )
    grad_normed1 = scatter_grads(
        jnp.einsum("stkh,dkh->std", grad_project, qkv_full, preferred_element_type=jnp.float32)
    )
    grad_norm_one, ln1_gain_part, ln1_bias_part = norm_backward(
        grad_normed1, centred1, inverse1, ln1_gain
    )
    grad_hidden0 = grad_hidden1 + grad_norm_one
    seq_sums = jnp.sum(grad_hidden0, axis=1)
    table_grad_full = jnp.einsum("sn,sd->nd", picked, seq_sums, precision=highest)
    vectors = lax.psum(
        (
            ln1_gain_part,
            ln1_bias_part,
            jnp.sum(grad_hidden1, axis=(0, 1)),
            ln2_gain_part,
            ln2_bias_part,
            jnp.sum(cotangent.astype(jnp.float32), axis=(0, 1)),
        ),
        ("dp", "row", "col"),
    )
    up_bias_grad = lax.psum(jnp.sum(grad_inner, axis=(0, 1)), ("dp", "col"))
    weights_full = (qkv_grad_full, out_grad_full, up_grad_full, down_grad_full)
    blocks = (
        lax.psum_scatter(
            weights_full[0].astype(jnp.bfloat16), "col", scatter_dimension=0, tiled=True
        ).astype(jnp.float32),
        lax.psum_scatter(
            weights_full[1].astype(jnp.bfloat16), "col", scatter_dimension=0, tiled=True
        ).astype(jnp.float32),
        lax.psum_scatter(
            weights_full[2].astype(jnp.bfloat16), "col", scatter_dimension=0, tiled=True
        ).astype(jnp.float32),
        lax.psum_scatter(
            weights_full[3].astype(jnp.bfloat16), "col", scatter_dimension=0, tiled=True
        ).astype(jnp.float32),
        lax.psum_scatter(
            table_grad_full.astype(jnp.bfloat16), "col", scatter_dimension=0, tiled=True
        ).astype(jnp.float32),
    )
    weight_blocks = (blocks[0], blocks[1], blocks[2], blocks[3])
    weight_blocks = (
        lax.psum(blocks[0].astype(jnp.bfloat16), "dp").astype(jnp.float32),
        lax.psum(blocks[1].astype(jnp.bfloat16), "dp").astype(jnp.float32),
        lax.psum(blocks[2].astype(jnp.bfloat16), "dp").astype(jnp.float32),
        lax.psum(blocks[3].astype(jnp.bfloat16), "dp").astype(jnp.float32),
    )
    table_block = lax.psum(blocks[4].astype(jnp.bfloat16), ("dp", "row")).astype(jnp.float32)
    return (
        result.astype(jnp.bfloat16),
        grad_hidden0,
        table_block,
        vectors[0],
        vectors[1],
        weight_blocks[0],
        weight_blocks[1],
        vectors[2],
        vectors[3],
        vectors[4],
        weight_blocks[2],
        up_bias_grad,
        weight_blocks[3],
        vectors[5],
    )


def solution(mesh):
    placed = (
        P(("dp", "col"), "row", None),
        P(("dp", "col"), "row", None),
        P(("dp", "col")),
        P(("dp", "col")),
        P("col", None),
        P(),
        P(),
        P("col", None, "row"),
        P("col", "row"),
        P(),
        P(),
        P(),
        P("col", "row"),
        P("row"),
        P("col", "row"),
        P(),
    )
    return jax.shard_map(
        body,
        mesh=mesh,
        in_specs=placed,
        out_specs=(
            P(("dp", "col"), "row", None),
            P(("dp", "col"), "row", None),
            P("col", None),
            P(),
            P(),
            P("col", None, "row"),
            P("col", "row"),
            P(),
            P(),
            P(),
            P("col", "row"),
            P("row"),
            P("col", "row"),
            P(),
        ),
        check_vma=False,
    )
```

profile of v0, /device:TPU:0, one launch (start us, length us, event | category | flops | bytes accessed | tf_op | source)
XLA Modules:
  0.0 882.5 jit_solution(11795420427352458064)
XLA Ops:
  8.7 13.4 %all-gather.21.cloned.1.call-done = bf16[2,500,768]{2,1,0:T(8,128)(2,1)} async-done(((bf16[1,500,768]{2,1,0:T(8,128)(2,1)}), bf16[2,500,768]{2,1,0:T(8,128)(2,1)}) %all-gather.21.cloned.1.call-update) | async-done | bytes 1536016 | tf_op jit(solution)/shard_map/all_gather | solution.py:151
  30.4 40.8 %all-gather.9.cloned.1.call-done = bf16[1,2048,768]{2,1,0:T(8,128)(2,1)} async-done(((bf16[1,512,768]{2,1,0:T(8,128)(2,1)}), bf16[1,2048,768]{2,1,0:T(8,128)(2,1)}) %all-gather.9.cloned.1.call-update) | async-done | bytes 3145744 | tf_op jit(solution)/shard_map/all_gather | solution.py:16
  75.7 91.3 %while.50 = (s32[]{:T(128)}, f32[4,512,3,64]{1,3,2,0:T(8,128)}, f32[4,3,512]{2,1,0:T(4,128)S(1)}, s32[4]{0:T(128)S(1)}, s32[]{:T(128)}, /*index=5*/bf16[2048,3,6...) while((s32[]{:T(128)}, f32[4,512,3,64]{1,3,2,0:T(8,128)}, ...), condition=%wide.region_5.6_spmd.clone.clone.clone, body=%wide.region_2.5_spmd.clone.clone.sunk.clone | while | flops 845153280 | bytes 44169396 | solution.py:76
  84.4 6.8 fusion.183
  91.2 7.4 fusion.184
  107.2 6.8 fusion.183
  114.0 7.4 fusion.184
  130.1 6.8 fusion.183
  136.8 7.4 fusion.184
  152.9 6.8 fusion.183
  159.6 7.3 fusion.184
  174.1 43.3 %reduce-scatter.17.cloned.1.call-done = bf16[1,512,768]{2,1,0:T(8,128)(2,1)} async-done(((bf16[1,2048,768]{2,1,0:T(8,128)(2,1)}), bf16[1,512,768]{2,1,0:T(8,128)(2,1)}) %reduce-scatter.17.cloned.1.call-update) | async-done | bytes 786448 | tf_op jit(solution)/shard_map/reduce_scatter | solution.py:20
  228.0 47.4 %all-gather.11.cloned.1.call-done = bf16[1,2048,768]{2,1,0:T(8,128)(2,1)} async-done(((bf16[1,512,768]{2,1,0:T(8,128)(2,1)}), bf16[1,2048,768]{2,1,0:T(8,128)(2,1)}) %all-gather.11.cloned.1.call-update) | async-done | bytes 3145744 | tf_op jit(solution)/shard_map/all_gather | solution.py:16
  275.4 19.0 %multiply_convert_fusion.1 = (bf16[2048,768]{1,0:T(8,128)(2,1)}, f32[2048,768]{1,0:T(8,128)}, f32[2048,768]{1,0:T(8,128)}) fusion(f32[768]{0:T(1024)S(1)} %copy-done.41, bf16[768,768]{1,0:T(8,128)(2,1)} %all-gather.13.cloned.1.call-done, bf16[1,2048,768]{2,1,0:T(8,128)(2,1)} %all-gather.11.cloned.1.call-done), kind=kOutput, calls=%fused_computation.54 | convolution fusion | flops 2519728128 | bytes 20057088 | tf_op jit(solution)/shard_map/std,df->stf/dot_general | solution.py:183
  294.4 38.7 %all-gather.17.cloned.1.call-done = bf16[1,2048,768]{2,1,0:T(8,128)(2,1)} async-done(((bf16[1,512,768]{2,1,0:T(8,128)(2,1)}), bf16[1,2048,768]{2,1,0:T(8,128)(2,1)}) %all-gather.17.cloned.1.call-update) | async-done | bytes 3145744 | tf_op jit(solution)/shard_map/all_gather | solution.py:26
  333.1 11.2 %fusion.112 = (f32[768]{0:T(1024)}, bf16[2048,768]{1,0:T(8,128)(2,1)S(1)}) fusion(f32[2048,768]{1,0:T(8,128)} %get-tuple-element.398, bf16[768,768]{1,0:T(8,128)(2,1)} %all-gather.15.cloned.1.call-done, bf16[1,2048,768]{2,1,0:T(8,128)(2,1)} %all-gather.17.cloned.1.call-done, f32[2048,768]{1,0:T(8,128)} %get-tuple-element.410, f32[768]{0:T(1024)S(1)} %copy-done.41), kind=kOutput, calls=%fused_computation.153 | convolution fusion | flops 2441084160 | bytes 20060160 | tf_op jit(solution)/shard_map/std,df->stf/dot_general | solution.py:229
  350.2 6.6 fusion.65
  356.9 37.2 %reduce-scatter.21.cloned.1.call-done = bf16[1,512,768]{2,1,0:T(8,128)(2,1)} async-done(((bf16[1,2048,768]{2,1,0:T(8,128)(2,1)}), bf16[1,512,768]{2,1,0:T(8,128)(2,1)}) %reduce-scatter.21.cloned.1.call-update) | async-done | bytes 786448 | tf_op jit(solution)/shard_map/reduce_scatter | solution.py:30
  396.8 44.2 %reduce-scatter.19.cloned.1.call-done = bf16[1,512,768]{2,1,0:T(8,128)(2,1)} async-done(((bf16[1,2048,768]{2,1,0:T(8,128)(2,1)}), bf16[1,512,768]{2,1,0:T(8,128)(2,1)}) %reduce-scatter.19.cloned.1.call-update) | async-done | bytes 786448 | tf_op jit(solution)/shard_map/reduce_scatter | solution.py:20
  448.5 6.5 fusion.100
  457.5 34.1 %all-gather.19.cloned.1.call-done = bf16[1,2048,768]{2,1,0:T(8,128)(2,1)} async-done(((bf16[1,512,768]{2,1,0:T(8,128)(2,1)}), bf16[1,2048,768]{2,1,0:T(8,128)(2,1)}) %all-gather.19.cloned.1.call-update) | async-done | bytes 3145744 | tf_op jit(solution)/shard_map/all_gather | solution.py:26
  501.2 87.8 %while.51 = (s32[]{:T(128)}, f32[2048,3,64]{0,2,1:T(8,128)S(1)}, f32[2048,3,64]{0,2,1:T(8,128)}, bf16[4,512,3,64]{1,3,2,0:T(8,128)(2,1)}, s32[4]{0:T(128)S(1)}, ...) while((s32[]{:T(128)}, f32[2048,3,64]{0,2,1:T(8,128)S(1)}, ...), condition=%wide.region_15.16_spmd.clone.clone.clone, body=%wide.region_14.15_spmd.clone.clone.sunk.clone | while | flops 2048887296 | bytes 79087952 | solution.py:121
  529.5 6.4 fusion.198
  551.5 6.4 fusion.198
  573.4 6.4 fusion.198
  601.8 6.8 fusion.92
  618.8 10.4 %reduce-scatter.25.cloned.1.call-done = bf16[384,768]{1,0:T(8,128)(2,1)} async-done(((bf16[768,768]{1,0:T(8,128)(2,1)}), bf16[384,768]{1,0:T(8,128)(2,1)}) %reduce-scatter.25.cloned.1.call-update) | async-done | bytes 589840 | tf_op jit(solution)/shard_map/reduce_scatter | solution.py:308
  629.3 48.0 %reduce-scatter.23.cloned.1.call-done = bf16[1,512,768]{2,1,0:T(8,128)(2,1)} async-done(((bf16[1,2048,768]{2,1,0:T(8,128)(2,1)}), bf16[1,512,768]{2,1,0:T(8,128)(2,1)}) %reduce-scatter.23.cloned.1.call-update) | async-done | bytes 786448 | tf_op jit(solution)/shard_map/reduce_scatter | solution.py:30
  693.0 18.3 %psum.93 = f32[768]{0:T(1024)} all-reduce(f32[768]{0:T(1024)S(1)} %copy-done.37), channel_id=1, replica_groups=mesh['dp'=4,'row'=4,'col'=2] {'dp','col'}, use_global_device_ids=true, to_apply=%region_39.40 | all-reduce | flops 768 | bytes 6144 | tf_op jit(solution)/shard_map/psum | solution.py:299
  711.3 46.5 %all-reduce.9.cloned.1.call-done = (bf16[384,768]{0,1:T(8,128)(2,1)}, bf16[384,3,192]{0,2,1:T(8,128)(2,1)}, bf16[384,192]{0,1:T(8,128)(2,1)}, bf16[384,768]{1,0:T(8,128)(2,1)}) async-done(((bf16[384,768]{0,1:T(8,128)(2,1)}, bf16[384,3,192]{0,2,1:T(8,128)(2,1)}, bf16[384,192]{0,1:T(8,128)(2,1)}, bf16[384,768]{1,0:T(8,128)(2,1)}), (bf16[384,768]{0,1:T(8,128)(2,1)}, bf16[384,3,192]{0,2,1:T(8,128)(2,1)}, ...) | async-done | bytes 1769488 | tf_op jit(solution)/shard_map/psum | solution.py:323
  765.0 40.0 %all-reduce.2 = (f32[768]{0:T(1024)}, f32[768]{0:T(1024)}, f32[768]{0:T(1024)}, f32[768]{0:T(1024)}, f32[768]{0:T(1024)}, /*index=5*/f32[768]{0:T(1024)}) all-reduce(f32[768]{0:T(1024)S(1)} %get-tuple-element.333, f32[768]{0:T(1024)S(1)} %get-tuple-element.342, ...), channel_id=1, replica_groups=mesh['dp'=4,'row'=4,'col'=2] {'dp','row','col'}, use_global_device_ids=true, to_apply=%region_23.24 | all-reduce | flops 4608 | bytes 36864 | tf_op jit(solution)/shard_map/psum | solution.py:288
  804.9 68.4 %all-reduce.7.cloned.1.call-done = bf16[500,768]{1,0:T(8,128)(2,1)} async-done(((bf16[500,768]{1,0:T(8,128)(2,1)}), bf16[500,768]{1,0:T(8,128)(2,1)}) %all-reduce.7.cloned.1.call-update) | async-done | bytes 768016 | tf_op jit(solution)/shard_map/psum | solution.py:325
  (275 shorter events, 195.8 us)
Async XLA Ops:
  7.2 14.9 %all-gather.21.cloned.1.call-start = ((), (), s32[]{:S(2)}) async-start(), calls=%async_computation.20 | async-start | bytes 2322432 | tf_op jit(solution)/shard_map/all_gather | solution.py:151
  7.9 63.2 %all-gather.9.cloned.1.call-start = ((), (), s32[]{:S(2)}) async-start(), calls=%async_computation.8 | async-start | bytes 3932160 | tf_op jit(solution)/shard_map/all_gather | solution.py:16
  24.1 416.9 %copy-start.19 = (f32[768]{0:T(1024)}, f32[768]{0:T(1024)S(1)}, u32[]{:S(2)}) copy-start(f32[768]{0:T(1024)S(1)} %convolution_reduce_fusion) | copy-start | bytes 9220
  24.6 50.5 %copy-start.26 = (f32[512]{0:T(512)}, f32[512]{0:T(512)S(1)}, u32[]{:S(2)}) copy-start(f32[512]{0:T(512)S(1)} %get-tuple-element.408) | copy-start | bytes 6148
  25.9 191.5 %reduce-scatter.17.cloned.1.call-start = ((), (), s32[]{:S(2)}) async-start(), calls=%async_computation.9 | async-start | bytes 3932160 | tf_op jit(solution)/shard_map/reduce_scatter | solution.py:20
  173.2 54.8 %all-gather.13.cloned.1.call-start = ((), (), s32[]{:S(2)}) async-start(), calls=%async_computation.11 | async-start | bytes 1769472 | tf_op jit(solution)/shard_map/all_gather | solution.py:149
  173.8 101.6 %copy-start.41 = (f32[768]{0:T(1024)S(1)}, f32[768]{0:T(1024)}, u32[]{:S(2)}) copy-start(f32[768]{0:T(1024)} %param.33) | copy-start | bytes 9220
  173.8 101.6 %all-gather.11.cloned.1.call-start = ((), (), s32[]{:S(2)}) async-start(), calls=%async_computation.10 | async-start | bytes 3932160 | tf_op jit(solution)/shard_map/all_gather | solution.py:16
  221.6 72.8 %all-gather.15.cloned.1.call-start = ((), (), s32[]{:S(2)}) async-start(), calls=%async_computation.12 | async-start | bytes 1769472 | tf_op jit(solution)/shard_map/all_gather | solution.py:150
  222.2 110.9 %all-gather.17.cloned.1.call-start = ((), (), s32[]{:S(2)}) async-start(), calls=%async_computation.14 | async-start | bytes 3932160 | tf_op jit(solution)/shard_map/all_gather | solution.py:26
  222.9 171.2 %reduce-scatter.21.cloned.1.call-start = ((), (), s32[]{:S(2)}) async-start(), calls=%async_computation.15 | async-start | bytes 3932160 | tf_op jit(solution)/shard_map/reduce_scatter | solution.py:30
  350.0 91.1 %reduce-scatter.19.cloned.1.call-start = ((), (), s32[]{:S(2)}) async-start(), calls=%async_computation.13 | async-start | bytes 3932160 | tf_op jit(solution)/shard_map/reduce_scatter | solution.py:20
  356.8 84.2 %copy-start.36 = (f32[768]{0:T(1024)S(1)}, f32[768]{0:T(1024)}, u32[]{:S(2)}) copy-start(f32[768]{0:T(1024)} %param.35) | copy-start | bytes 9220
  356.9 134.8 %all-gather.19.cloned.1.call-start = ((), (), s32[]{:S(2)}) async-start(), calls=%async_computation.16 | async-start | bytes 3932160 | tf_op jit(solution)/shard_map/all_gather | solution.py:26
  447.5 165.3 %reduce-scatter.31.cloned.1.call-start = ((), (), s32[]{:S(2)}) async-start(), calls=%async_computation.23 | async-start | bytes 1769472
  457.5 157.6 %reduce-scatter.29.cloned.1.call-start = ((), (), s32[]{:S(2)}) async-start(), calls=%async_computation.22 | async-start | bytes 589824
  596.3 20.5 %reduce-scatter.27.cloned.1.call-start = ((), (), s32[]{:S(2)}) async-start(), calls=%async_computation.21 | async-start | bytes 1474560
  601.7 27.5 %reduce-scatter.25.cloned.1.call-start = ((), (), s32[]{:S(2)}) async-start(), calls=%async_computation.19 | async-start | bytes 1769472 | tf_op jit(solution)/shard_map/reduce_scatter | solution.py:308
  608.5 68.7 %reduce-scatter.23.cloned.1.call-start = ((), (), s32[]{:S(2)}) async-start(), calls=%async_computation.17 | async-start | bytes 3932160 | tf_op jit(solution)/shard_map/reduce_scatter | solution.py:30
  612.7 64.6 %copy-start.1 = (bf16[1,512,768]{2,1,0:T(8,128)(2,1)S(1)}, bf16[1,512,768]{2,1,0:T(8,128)(2,1)}, u32[]{:S(2)}) copy-start(bf16[1,512,768]{2,1,0:T(8,128)(2,1)} %param.20) | copy-start | bytes 2359300
  612.7 64.6 %copy-start.20 = (f32[768]{0:T(1024)S(1)}, f32[768]{0:T(1024)}, u32[]{:S(2)}) copy-start(f32[768]{0:T(1024)} %copy-done.19) | copy-start | bytes 9220
  612.7 64.6 %copy-start.25 = (f32[768]{0:T(1024)S(1)}, f32[768]{0:T(1024)}, u32[]{:S(2)}) copy-start(f32[768]{0:T(1024)} %param.25) | copy-start | bytes 9220
  612.7 64.6 %copy-start.27 = (f32[512]{0:T(512)S(1)}, f32[512]{0:T(512)}, u32[]{:S(2)}) copy-start(f32[512]{0:T(512)} %copy-done.26) | copy-start | bytes 6148
  612.7 64.6 %copy-start.29 = (f32[512]{0:T(512)S(1)}, f32[512]{0:T(512)}, u32[]{:S(2)}) copy-start(f32[512]{0:T(512)} %copy-done.28) | copy-start | bytes 6148
  612.7 66.6 %copy-start.3 = (f32[1,512,768]{2,1,0:T(8,128)S(1)}, f32[1,512,768]{2,1,0:T(8,128)}, u32[]{:S(2)}) copy-start(f32[1,512,768]{2,1,0:T(8,128)} %copy-done.2) | copy-start | bytes 4718596
  612.7 145.1 %all-reduce.9.cloned.1.call-start = ((), (), s32[]{:S(2)}) async-start(), calls=%async_computation.24 | async-start | bytes 3538944 | tf_op jit(solution)/shard_map/psum | solution.py:323
  629.3 244.1 %all-reduce.7.cloned.1.call-start = ((), (), s32[]{:S(2)}) async-start(), calls=%async_computation.18 | async-start | bytes 1548288 | tf_op jit(solution)/shard_map/psum | solution.py:325
  686.9 3.5 collective-permute-start
  693.0 72.0 %copy-start.30 = (f32[768]{0:T(1024)S(1)}, f32[768]{0:T(1024)}, u32[]{:S(2)}) copy-start(f32[768]{0:T(1024)} %get-tuple-element.331) | copy-start | bytes 9220
  693.0 72.0 %copy-start.31 = (f32[768]{0:T(1024)S(1)}, f32[768]{0:T(1024)}, u32[]{:S(2)}) copy-start(f32[768]{0:T(1024)} %get-tuple-element.341) | copy-start | bytes 9220
  693.0 72.0 %copy-start.32 = (f32[768]{0:T(1024)S(1)}, f32[768]{0:T(1024)}, u32[]{:S(2)}) copy-start(f32[768]{0:T(1024)} %get-tuple-element.393) | copy-start | bytes 9220
  693.0 72.0 %copy-start.33 = (f32[768]{0:T(1024)S(1)}, f32[768]{0:T(1024)}, u32[]{:S(2)}) copy-start(f32[768]{0:T(1024)} %get-tuple-element.405) | copy-start | bytes 9220
  (38 other events, 475.0 us)
Sparse Core Ops, SparseCore 0:
  9.6 12.4 all-gather.20
  26.0 45.1 all-gather.8
  173.4 43.9 reduce-scatter.16
  218.8 9.1 all-gather.12
  230.3 45.1 all-gather.10
  276.8 9.2 all-gather.14
  287.9 45.1 all-gather.16
  350.1 43.9 reduce-scatter.20
  397.1 43.9 reduce-scatter.18
  447.6 43.9 all-gather.18
  494.4 8.6 reduce-scatter.30
  596.4 7.6 reduce-scatter.28
  606.9 9.6 reduce-scatter.26
  619.4 9.8 reduce-scatter.24
  632.1 45.1 reduce-scatter.22
  680.9 76.8 all-reduce.8
  764.4 108.9 all-reduce.6
where the time goes:
time: 892 us; the launch traced here: 882 us
  waiting for transfers between devices  480 us (54%)
  matrix products  196 us (22%)
  other arithmetic  72.5 us (8%)
  blocking collectives  67.1 us (8%)
  local copies, waits for them, and re-layouts  33.4 us (4%)
  between operations  16.1 us (2%)
  loops' own time  14.2 us (2%)
    all_gather x2, waiting for transfers between devices, gather_rows(): return lax.all_gather(values, 'row', axis=1, tiled=True)  88.2 us
    reduce_scatter x2, waiting for transfers between devices, scatter_rows(): lax.psum_scatter(values.astype(jnp.bfloat16), 'row', scatter_dimension=1,...  87.5 us
    reduce_scatter x2, waiting for transfers between devices, scatter_grads(): lax.psum_scatter(values.astype(jnp.bfloat16), 'row', scatter_dimension=1,...  85.2 us
    all_gather x2, waiting for transfers between devices, gather_grads(): return lax.all_gather(values, 'row', axis=1, tiled=True)  72.8 us
    psum x1, waiting for transfers between devices, body(): lax.psum(blocks[4].astype(jnp.bfloat16), ('dp', 'row')).astype(jnp.float32)  68.4 us
    psum x1, waiting for transfers between devices, body(): lax.psum(blocks[3].astype(jnp.bfloat16), 'dp').astype(jnp.float32)  46.5 us
    psum x1, blocking collectives, body(): lax.psum((ln1_gain_part, ln1_bias_part, jnp.sum(grad_hidden1, axis=(0, 1)...  40 us
    dot_general x8, matrix products, one_block(): jnp.einsum('qhd,khd->hqk', query_blk, key_rows, preferred_element_type=jn...  31.4 us
  transfers between devices with their start and end apart: 18, of which 13 were waited for; matrix products, arithmetic and copies ran while one was open for 20% of the time, Pallas kernels for 0%

commit v1 on v0

--- a/solution.py
+++ b/solution.py
@@ -8,12 +8,34 @@
 masked_score = -1e30
 
 
+def laid_out(blocks, dim):
+    dims = list(blocks.shape[1:])
+    dims[dim] *= blocks.shape[0]
+    return jnp.moveaxis(blocks, 0, dim).reshape(dims)
+
+
+def collected_by_bits(x, axis):
+    size = lax.axis_size(axis)
+    tiles = x[None]
+    for level in range(size.bit_length() - 1):
+        stride = 1 << level
+        received = lax.ppermute(tiles, axis, [(i, i ^ stride) for i in range(size)])
+        both = jnp.stack([tiles, received])
+        upper = lax.axis_index(axis) >> level & 1
+        tiles = jnp.where(upper == 0, both, both[::-1]).reshape(-1, *x.shape)
+    return tiles
+
+
+def doubled_up(value, axis, dim):
+    return laid_out(collected_by_bits(value, axis), dim)
+
+
 def gelu_exact(values):
     return jax.nn.gelu(values, approximate=False)
 
 
 def gather_rows(values):
-    return lax.all_gather(values, "row", axis=1, tiled=True)
+    return doubled_up(values, "row", 1)
 
 
 def scatter_rows(values):

time: 892 us -> 874 us (0.980)
  waiting for transfers between devices: 480 us -> 456 us
  other arithmetic: 72.5 us -> 82.4 us
    ppermute x0 -> x4, waiting for transfers between devices: none -> 107 us  [collected_by_bits(): received = lax.ppermute(tiles, axis, [(i, i ^ stride) for i in range(size)])]
    all_gather x2 -> x0, waiting for transfers between devices: 88.2 us -> none  [gather_rows(): return lax.all_gather(values, 'row', axis=1, tiled=True)]
    all_gather x2, waiting for transfers between devices: 72.8 us -> 34.1 us  [gather_grads(): return lax.all_gather(values, 'row', axis=1, tiled=True)]
    another operation x5 -> x13, other arithmetic: 2.06 us -> 11.7 us  [the longest x8 9.66 us: collected_by_bits(): both = jnp.stack([tiles, received])]
    unnamed x93 -> x95, local copies, waits for them, and re-layouts: 23.4 us -> 23.7 us
  transfers between devices with their start and end apart: 18 -> 20, of which waited for: 13 -> 13; matrix products, arithmetic and copies ran while one was open for 20% -> 21% of each run, Pallas kernels for 0% -> 0%
where the time goes in v1:
time: 874 us; the launch traced here: 870 us
  waiting for transfers between devices  456 us (52%)
  matrix products  191 us (22%)
  other arithmetic  82.4 us (9%)
  blocking collectives  67.7 us (8%)
  local copies, waits for them, and re-layouts  34.6 us (4%)
  between operations  16.1 us (2%)
  loops' own time  12.6 us (1%)
  starting transfers between devices  9.86 us (1%)
    ppermute x4, waiting for transfers between devices, collected_by_bits(): received = lax.ppermute(tiles, axis, [(i, i ^ stride) for i in range(size)])  107 us
    reduce_scatter x2, waiting for transfers between devices, scatter_rows(): lax.psum_scatter(values.astype(jnp.bfloat16), 'row', scatter_dimension=1,...  89.5 us
    reduce_scatter x2, waiting for transfers between devices, scatter_grads(): lax.psum_scatter(values.astype(jnp.bfloat16), 'row', scatter_dimension=1,...  85.2 us
    psum x1, waiting for transfers between devices, body(): lax.psum(blocks[4].astype(jnp.bfloat16), ('dp', 'row')).astype(jnp.float32)  68.4 us
    psum x1, waiting for transfers between devices, body(): lax.psum(blocks[3].astype(jnp.bfloat16), 'dp').astype(jnp.float32)  46.5 us
    psum x1, blocking collectives, body(): lax.psum((ln1_gain_part, ln1_bias_part, jnp.sum(grad_hidden1, axis=(0, 1)...  40 us
    all_gather x2, waiting for transfers between devices, gather_grads(): return lax.all_gather(values, 'row', axis=1, tiled=True)  34.1 us
    dot_general x8, matrix products, one_block(): jnp.einsum('qhd,khd->hqk', query_blk, key_rows, preferred_element_type=jn...  31.3 us
  transfers between devices with their start and end apart: 20, of which 13 were waited for; matrix products, arithmetic and copies ran while one was open for 21% of the time, Pallas kernels for 0%

profile of v1, /device:TPU:0, one launch (start us, length us, event | category | flops | bytes accessed | tf_op | source)
XLA Modules:
  0.0 869.7 jit_solution(2679915666197426648)
XLA Ops:
  8.7 13.4 %all-gather.15.cloned.1.call-done = bf16[2,500,768]{2,1,0:T(8,128)(2,1)} async-done(((bf16[1,500,768]{2,1,0:T(8,128)(2,1)}), bf16[2,500,768]{2,1,0:T(8,128)(2,1)}) %all-gather.15.cloned.1.call-update) | async-done | bytes 1536016 | tf_op jit(solution)/shard_map/all_gather | solution.py:173
  26.8 18.0 %collective-permute-done = bf16[1,1,512,768]{3,2,1,0:T(8,128)(2,1)S(1)} collective-permute-done((bf16[1,1,512,768]{3,2,1,0:T(8,128)(2,1)S(1)}, bf16[1,1,512,768]{3,2,1,0:T(8,128)(2,1)S(1)}, u32[]{:S(2)}, u32[]{:S(2)}) %collective-permute-start) | collective-permute-done | bytes 786464 | tf_op jit(solution)/shard_map/ppermute | solution.py:22
  53.3 29.3 %collective-permute-done.1 = bf16[2,1,512,768]{3,2,0,1:T(8,128)(2,1)} collective-permute-done((bf16[2,1,512,768]{3,2,0,1:T(8,128)(2,1)}, bf16[2,1,512,768]{3,2,0,1:T(8,128)(2,1)}, u32[]{:S(2)}, u32[]{:S(2)}) %collective-permute-start.1) | collective-permute-done | bytes 1572896 | tf_op jit(solution)/shard_map/ppermute | solution.py:22
  88.3 89.1 %while.50 = (s32[]{:T(128)}, f32[4,512,3,64]{1,3,2,0:T(8,128)S(1)}, f32[4,3,512]{2,1,0:T(4,128)S(1)}, s32[4]{0:T(128)S(1)}, s32[]{:T(128)}, /*index=5*/bf16[2048...) while((s32[]{:T(128)}, f32[4,512,3,64]{1,3,2,0:T(8,128)S(1)}, ...), condition=%wide.region_5.6_spmd.clone.clone.clone, body=%wide.region_2.5_spmd.clone.clone.sunk.clone | while | flops 845153280 | bytes 47319244 | solution.py:98
  97.0 6.8 fusion.188
  103.8 6.8 fusion.189
  119.3 6.8 fusion.188
  126.1 6.8 fusion.189
  141.5 6.8 fusion.188
  148.4 6.8 fusion.189
  163.8 6.8 fusion.188
  170.7 6.8 fusion.189
  182.4 45.2 %reduce-scatter.17.cloned.1.call-done = bf16[1,512,768]{2,1,0:T(8,128)(2,1)} async-done(((bf16[1,2048,768]{2,1,0:T(8,128)(2,1)}), bf16[1,512,768]{2,1,0:T(8,128)(2,1)}) %reduce-scatter.17.cloned.1.call-update) | async-done | bytes 786448 | tf_op jit(solution)/shard_map/reduce_scatter | solution.py:42
  234.2 17.4 %collective-permute-done.2 = bf16[1,1,512,768]{3,2,1,0:T(8,128)(2,1)} collective-permute-done((bf16[1,1,512,768]{3,2,1,0:T(8,128)(2,1)}, bf16[1,1,512,768]{3,2,1,0:T(8,128)(2,1)}, u32[]{:S(2)}, u32[]{:S(2)}) %collective-permute-start.2) | collective-permute-done | bytes 786464 | tf_op jit(solution)/shard_map/ppermute | solution.py:22
  256.9 41.9 %collective-permute-done.3 = bf16[2,1,512,768]{3,2,0,1:T(8,128)(2,1)} collective-permute-done((bf16[2,1,512,768]{3,2,0,1:T(8,128)(2,1)}, bf16[2,1,512,768]{3,2,0,1:T(8,128)(2,1)}, u32[]{:S(2)}, u32[]{:S(2)}) %collective-permute-start.3) | collective-permute-done | bytes 1572896 | tf_op jit(solution)/shard_map/ppermute | solution.py:22
  303.2 19.0 %multiply_convert_fusion.1 = (bf16[2048,768]{1,0:T(8,128)(2,1)}, f32[2048,768]{1,0:T(8,128)}, f32[2048,768]{1,0:T(8,128)}) fusion(f32[768]{0:T(1024)S(1)} %copy-done.43, bf16[2048,768]{1,0:T(8,128)(2,1)} %bitcast.214, bf16[768,768]{1,0:T(8,128)(2,1)} %all-gather.7.cloned.1.call-done), kind=kOutput, calls=%fused_computation.54 | convolution fusion | flops 2519728128 | bytes 20057088 | tf_op jit(solution)/shard_map/std,df->stf/dot_general | solution.py:205
  322.2 11.2 %fusion.109 = (f32[768]{0:T(1024)}, bf16[2048,768]{1,0:T(8,128)(2,1)S(1)}) fusion(f32[2048,768]{1,0:T(8,128)} %get-tuple-element.398, bf16[768,768]{1,0:T(8,128)(2,1)} %all-gather.9.cloned.1.call-done, bf16[1,2048,768]{2,1,0:T(8,128)(2,1)} %all-gather.11.cloned.1.call-done, f32[2048,768]{1,0:T(8,128)} %get-tuple-element.416, f32[768]{0:T(1024)S(1)} %copy-done.43), kind=kOutput, calls=%fused_computation.160 | convolution fusion | flops 2441084160 | bytes 20060160 | tf_op jit(solution)/shard_map/std,df->stf/dot_general | solution.py:251
  339.6 6.6 fusion.57
  346.2 37.1 %reduce-scatter.21.cloned.1.call-done = bf16[1,512,768]{2,1,0:T(8,128)(2,1)} async-done(((bf16[1,2048,768]{2,1,0:T(8,128)(2,1)}), bf16[1,512,768]{2,1,0:T(8,128)(2,1)}) %reduce-scatter.21.cloned.1.call-update) | async-done | bytes 786448 | tf_op jit(solution)/shard_map/reduce_scatter | solution.py:52
  386.0 44.2 %reduce-scatter.19.cloned.1.call-done = bf16[1,512,768]{2,1,0:T(8,128)(2,1)} async-done(((bf16[1,2048,768]{2,1,0:T(8,128)(2,1)}), bf16[1,512,768]{2,1,0:T(8,128)(2,1)}) %reduce-scatter.19.cloned.1.call-update) | async-done | bytes 786448 | tf_op jit(solution)/shard_map/reduce_scatter | solution.py:42
  437.6 6.5 fusion.91
  446.6 34.1 %all-gather.13.cloned.1.call-done = bf16[1,2048,768]{2,1,0:T(8,128)(2,1)} async-done(((bf16[1,512,768]{2,1,0:T(8,128)(2,1)}), bf16[1,2048,768]{2,1,0:T(8,128)(2,1)}) %all-gather.13.cloned.1.call-update) | async-done | bytes 3145744 | tf_op jit(solution)/shard_map/all_gather | solution.py:48
  490.4 85.8 %while.51 = (s32[]{:T(128)}, f32[2048,3,64]{0,2,1:T(8,128)S(1)}, f32[2048,3,64]{0,2,1:T(8,128)}, bf16[4,512,3,64]{1,3,2,0:T(8,128)(2,1)}, s32[4]{0:T(128)S(1)}, ...) while((s32[]{:T(128)}, f32[2048,3,64]{0,2,1:T(8,128)S(1)}, ...), condition=%wide.region_15.16_spmd.clone.clone.clone, body=%wide.region_14.15_spmd.clone.clone.sunk.clone | while | flops 2048887296 | bytes 79087952 | solution.py:143
  517.6 6.3 fusion.203
  539.1 6.3 fusion.203
  588.8 6.8 fusion.85
  605.9 10.4 %reduce-scatter.25.cloned.1.call-done = bf16[384,768]{1,0:T(8,128)(2,1)} async-done(((bf16[768,768]{1,0:T(8,128)(2,1)}), bf16[384,768]{1,0:T(8,128)(2,1)}) %reduce-scatter.25.cloned.1.call-update) | async-done | bytes 589840 | tf_op jit(solution)/shard_map/reduce_scatter | solution.py:330
  616.4 48.1 %reduce-scatter.23.cloned.1.call-done = bf16[1,512,768]{2,1,0:T(8,128)(2,1)} async-done(((bf16[1,2048,768]{2,1,0:T(8,128)(2,1)}), bf16[1,512,768]{2,1,0:T(8,128)(2,1)}) %reduce-scatter.23.cloned.1.call-update) | async-done | bytes 786448 | tf_op jit(solution)/shard_map/reduce_scatter | solution.py:52
  680.2 18.3 %psum.93 = f32[768]{0:T(1024)} all-reduce(f32[768]{0:T(1024)S(1)} %copy-done.40), channel_id=1, replica_groups=mesh['dp'=4,'row'=4,'col'=2] {'dp','col'}, use_global_device_ids=true, to_apply=%region_39.40 | all-reduce | flops 768 | bytes 6144 | tf_op jit(solution)/shard_map/psum | solution.py:321
  698.5 46.5 %all-reduce.9.cloned.1.call-done = (bf16[384,768]{0,1:T(8,128)(2,1)}, bf16[384,3,192]{0,2,1:T(8,128)(2,1)}, bf16[384,192]{0,1:T(8,128)(2,1)}, bf16[384,768]{1,0:T(8,128)(2,1)}) async-done(((bf16[384,768]{0,1:T(8,128)(2,1)}, bf16[384,3,192]{0,2,1:T(8,128)(2,1)}, bf16[384,192]{0,1:T(8,128)(2,1)}, bf16[384,768]{1,0:T(8,128)(2,1)}), (bf16[384,768]{0,1:T(8,128)(2,1)}, bf16[384,3,192]{0,2,1:T(8,128)(2,1)}, ...) | async-done | bytes 1769488 | tf_op jit(solution)/shard_map/psum | solution.py:345
  752.2 40.0 %all-reduce.2 = (f32[768]{0:T(1024)}, f32[768]{0:T(1024)}, f32[768]{0:T(1024)}, f32[768]{0:T(1024)}, f32[768]{0:T(1024)}, /*index=5*/f32[768]{0:T(1024)}) all-reduce(f32[768]{0:T(1024)S(1)} %get-tuple-element.333, f32[768]{0:T(1024)S(1)} %get-tuple-element.342, ...), channel_id=1, replica_groups=mesh['dp'=4,'row'=4,'col'=2] {'dp','row','col'}, use_global_device_ids=true, to_apply=%region_23.24 | all-reduce | flops 4608 | bytes 36864 | tf_op jit(solution)/shard_map/psum | solution.py:310
  792.1 68.4 %all-reduce.7.cloned.1.call-done = bf16[500,768]{1,0:T(8,128)(2,1)} async-done(((bf16[500,768]{1,0:T(8,128)(2,1)}), bf16[500,768]{1,0:T(8,128)(2,1)}) %all-reduce.7.cloned.1.call-update) | async-done | bytes 768016 | tf_op jit(solution)/shard_map/psum | solution.py:347
  (296 shorter events, 211.7 us)
Async XLA Ops:
  7.2 14.9 %all-gather.15.cloned.1.call-start = ((), (), s32[]{:S(2)}) async-start(), calls=%async_computation.18 | async-start | bytes 2322432 | tf_op jit(solution)/shard_map/all_gather | solution.py:173
  7.9 219.7 %reduce-scatter.17.cloned.1.call-start = ((), (), s32[]{:S(2)}) async-start(), calls=%async_computation.8 | async-start | bytes 3932160 | tf_op jit(solution)/shard_map/reduce_scatter | solution.py:42
  25.0 19.8 %collective-permute-start = (bf16[1,1,512,768]{3,2,1,0:T(8,128)(2,1)S(1)}, bf16[1,1,512,768]{3,2,1,0:T(8,128)(2,1)S(1)}, u32[]{:S(2)}, u32[]{:S(2)}) collective-permute-start(bf16[1,1,512,768]{3,2,1,0:T(8,128)(2,1)S(1)} %get-tuple-element.410), channel_id=1, source_target_pairs={{0,2},{2,0},{4,6},{6,4},{1,3},{3,1},{5,7},{7,5},{8,10},{10,8},{12,... | collective-permute-start | bytes 2359304 | tf_op jit(solution)/shard_map/ppermute | solution.py:22
  46.4 36.1 %collective-permute-start.1 = (bf16[2,1,512,768]{3,2,0,1:T(8,128)(2,1)}, bf16[2,1,512,768]{3,2,0,1:T(8,128)(2,1)}, u32[]{:S(2)}, u32[]{:S(2)}) collective-permute-start(bf16[2,1,512,768]{3,2,0,1:T(8,128)(2,1)} %get-tuple-element.408), channel_id=1, source_target_pairs={{0,4},{2,6},{4,0},{6,2},{1,5},{3,7},{5,1},{7,3},{8,12},{10,14},{12... | collective-permute-start | bytes 4718600 | tf_op jit(solution)/shard_map/ppermute | solution.py:22
  179.6 48.0 %copy-start.25 = (f32[768]{0:T(1024)S(1)}, f32[768]{0:T(1024)}, u32[]{:S(2)}) copy-start(f32[768]{0:T(1024)} %param.29) | copy-start | bytes 9220
  182.4 120.9 %all-gather.7.cloned.1.call-start = ((), (), s32[]{:S(2)}) async-start(), calls=%async_computation.9 | async-start | bytes 1769472 | tf_op jit(solution)/shard_map/all_gather | solution.py:171
  231.9 19.6 %collective-permute-start.2 = (bf16[1,1,512,768]{3,2,1,0:T(8,128)(2,1)}, bf16[1,1,512,768]{3,2,1,0:T(8,128)(2,1)}, u32[]{:S(2)}, u32[]{:S(2)}) collective-permute-start(bf16[1,1,512,768]{3,2,1,0:T(8,128)(2,1)} %fusion.141), channel_id=1, source_target_pairs={{0,2},{2,0},{4,6},{6,4},{1,3},{3,1},{5,7},{7,5},{8,10},{10,8},{12,... | collective-permute-start | bytes 2359304 | tf_op jit(solution)/shard_map/ppermute | solution.py:22
  233.4 88.8 %all-gather.9.cloned.1.call-start = ((), (), s32[]{:S(2)}) async-start(), calls=%async_computation.10 | async-start | bytes 1769472 | tf_op jit(solution)/shard_map/all_gather | solution.py:172
  254.8 44.0 %collective-permute-start.3 = (bf16[2,1,512,768]{3,2,0,1:T(8,128)(2,1)}, bf16[2,1,512,768]{3,2,0,1:T(8,128)(2,1)}, u32[]{:S(2)}, u32[]{:S(2)}) collective-permute-start(bf16[2,1,512,768]{3,2,0,1:T(8,128)(2,1)} %get-tuple-element.406), channel_id=1, source_target_pairs={{0,4},{2,6},{4,0},{6,2},{1,5},{3,7},{5,1},{7,3},{8,12},{10,14},{12... | collective-permute-start | bytes 4718600 | tf_op jit(solution)/shard_map/ppermute | solution.py:22
  256.2 66.0 %all-gather.11.cloned.1.call-start = ((), (), s32[]{:S(2)}) async-start(), calls=%async_computation.12 | async-start | bytes 3932160 | tf_op jit(solution)/shard_map/all_gather | solution.py:48
  256.8 126.5 %reduce-scatter.21.cloned.1.call-start = ((), (), s32[]{:S(2)}) async-start(), calls=%async_computation.13 | async-start | bytes 3932160 | tf_op jit(solution)/shard_map/reduce_scatter | solution.py:52
  339.1 91.1 %reduce-scatter.19.cloned.1.call-start = ((), (), s32[]{:S(2)}) async-start(), calls=%async_computation.11 | async-start | bytes 3932160 | tf_op jit(solution)/shard_map/reduce_scatter | solution.py:42
  346.1 84.1 %copy-start.39 = (f32[768]{0:T(1024)S(1)}, f32[768]{0:T(1024)}, u32[]{:S(2)}) copy-start(f32[768]{0:T(1024)} %param.35) | copy-start | bytes 9220
  346.2 134.5 %all-gather.13.cloned.1.call-start = ((), (), s32[]{:S(2)}) async-start(), calls=%async_computation.14 | async-start | bytes 3932160 | tf_op jit(solution)/shard_map/all_gather | solution.py:48
  436.6 163.3 %reduce-scatter.31.cloned.1.call-start = ((), (), s32[]{:S(2)}) async-start(), calls=%async_computation.21 | async-start | bytes 1769472
  446.6 155.6 %reduce-scatter.29.cloned.1.call-start = ((), (), s32[]{:S(2)}) async-start(), calls=%async_computation.20 | async-start | bytes 589824
  583.4 20.5 %reduce-scatter.27.cloned.1.call-start = ((), (), s32[]{:S(2)}) async-start(), calls=%async_computation.19 | async-start | bytes 1474560
  588.8 27.5 %reduce-scatter.25.cloned.1.call-start = ((), (), s32[]{:S(2)}) async-start(), calls=%async_computation.17 | async-start | bytes 1769472 | tf_op jit(solution)/shard_map/reduce_scatter | solution.py:330
  595.6 68.8 %reduce-scatter.23.cloned.1.call-start = ((), (), s32[]{:S(2)}) async-start(), calls=%async_computation.15 | async-start | bytes 3932160 | tf_op jit(solution)/shard_map/reduce_scatter | solution.py:52
  599.7 64.7 %copy-start.2 = (bf16[1,512,768]{2,1,0:T(8,128)(2,1)S(1)}, bf16[1,512,768]{2,1,0:T(8,128)(2,1)}, u32[]{:S(2)}) copy-start(bf16[1,512,768]{2,1,0:T(8,128)(2,1)} %param.20) | copy-start | bytes 2359300
  599.7 64.7 %copy-start.24 = (f32[768]{0:T(1024)S(1)}, f32[768]{0:T(1024)}, u32[]{:S(2)}) copy-start(f32[768]{0:T(1024)} %copy-done.22) | copy-start | bytes 9220
  599.7 64.7 %copy-start.28 = (f32[768]{0:T(1024)S(1)}, f32[768]{0:T(1024)}, u32[]{:S(2)}) copy-start(f32[768]{0:T(1024)} %param.25) | copy-start | bytes 9220
  599.7 64.7 %copy-start.30 = (f32[512]{0:T(512)S(1)}, f32[512]{0:T(512)}, u32[]{:S(2)}) copy-start(f32[512]{0:T(512)} %copy-done.29) | copy-start | bytes 6148
  599.8 64.7 %copy-start.32 = (f32[512]{0:T(512)S(1)}, f32[512]{0:T(512)}, u32[]{:S(2)}) copy-start(f32[512]{0:T(512)} %copy-done.31) | copy-start | bytes 6148
  599.8 66.7 %copy-start.5 = (f32[1,512,768]{2,1,0:T(8,128)S(1)}, f32[1,512,768]{2,1,0:T(8,128)}, u32[]{:S(2)}) copy-start(f32[1,512,768]{2,1,0:T(8,128)} %copy-done.4) | copy-start | bytes 4718596
  599.8 145.2 %all-reduce.9.cloned.1.call-start = ((), (), s32[]{:S(2)}) async-start(), calls=%async_computation.22 | async-start | bytes 3538944 | tf_op jit(solution)/shard_map/psum | solution.py:345
  616.3 244.2 %all-reduce.7.cloned.1.call-start = ((), (), s32[]{:S(2)}) async-start(), calls=%async_computation.16 | async-start | bytes 1548288 | tf_op jit(solution)/shard_map/psum | solution.py:347
  674.1 3.5 collective-permute-start.4
  680.2 72.0 %copy-start.34 = (f32[768]{0:T(1024)S(1)}, f32[768]{0:T(1024)}, u32[]{:S(2)}) copy-start(f32[768]{0:T(1024)} %get-tuple-element.331) | copy-start | bytes 9220
  680.2 72.0 %copy-start.35 = (f32[768]{0:T(1024)S(1)}, f32[768]{0:T(1024)}, u32[]{:S(2)}) copy-start(f32[768]{0:T(1024)} %get-tuple-element.341) | copy-start | bytes 9220
  680.2 72.0 %copy-start.36 = (f32[768]{0:T(1024)S(1)}, f32[768]{0:T(1024)}, u32[]{:S(2)}) copy-start(f32[768]{0:T(1024)} %get-tuple-element.393) | copy-start | bytes 9220
  680.2 72.0 %copy-start.37 = (f32[768]{0:T(1024)S(1)}, f32[768]{0:T(1024)}, u32[]{:S(2)}) copy-start(f32[768]{0:T(1024)} %get-tuple-element.411) | copy-start | bytes 9220
  (45 other events, 446.3 us)
Sparse Core Ops, SparseCore 0:
  9.6 12.4 all-gather.14
  182.5 45.1 reduce-scatter.16
  233.5 9.2 all-gather.6
  256.3 9.2 all-gather.8
  267.3 53.6 all-gather.10
  339.2 44.0 reduce-scatter.20
  386.3 43.9 reduce-scatter.18
  436.7 43.9 all-gather.12
  483.5 8.6 reduce-scatter.30
  583.5 7.6 reduce-scatter.28
  594.0 9.6 reduce-scatter.26
  606.5 9.8 reduce-scatter.24
  619.3 45.1 reduce-scatter.22
  668.1 76.8 all-reduce.8
  751.6 108.9 all-reduce.6
